TPU v7x, 512 devices: a whole 4x4x16 slice. The times are simulated.
512 devices in a mesh: gx: 32 (over x, y, core), gy: 16 (over z).
Axes of the slice: x: 4, y: 4, z: 16, core: 2. Of those that a mesh axis runs over, the one named last changes fastest.
Arguments:
- schur_blocks: float32 [32, 16, 768, 768], P('gx', 'gy'), may hold values from -32 to 32, as said below
- basis: float32 [32, 16, 32, 768], P('gx', 'gy'), may hold values from -0.21875 to 0.21875
- loads: float32 [32, 16, 16, 768], P('gx', 'gy'), may hold values from -64 to 64
- coarse_inverse: float32 [16384, 16384], P(('gx', 'gy')), may hold values from -0.09375 to 0.09375
- iface_map: int32 [32, 16, 768], P('gx', 'gy'), may hold values from 0 to 767, as said below
- coarse_slot: int32 [512], replicated, may hold values from 0 to 511, each once
Outputs:
- solution: float32 [32, 16, 16, 768], P('gx', 'gy')
Inputs may be any that keep to these rules, and one draw needn't show every extreme that they name: `schur_blocks`: each block is symmetric. `iface_map`: for every subdomain the map is a permutation of 0 to 767 that maps each aligned block of 128 cells onto itself. `coarse_slot`: every subdomain has its own coarse block number.
All inputs are finite; a program needn't handle non-finite values.
Results may differ from a plain program's by a relative error of at most 0.0001.
Values sent between devices are 32-bit elements; how exact they have to be, the bound alone decides.
No kernel may reach another device: no remote copies, remote signals or barrier semaphores. Data moves between devices by JAX's collectives and lax.ppermute only.
A program may use at most 128 MiB of HBM per device.

v0:
```python
import jax
import jax.numpy as jnp
from jax import lax
from jax.sharding import PartitionSpec as P

EW = 256
ES = 128
ITERS = 3
highest = lax.Precision.HIGHEST
epsilon = 1e-06


def padded(block, sides, width):
    for axis, dim in sides:
        count = lax.axis_size(axis)
        forward = [(i, i + 1) for i in range(count - 1)]
        backward = [(target, source) for source, target in forward]
        low = lax.ppermute(
            lax.slice_in_dim(block, block.shape[dim] - width, None, axis=dim), axis, forward
        )
        high = lax.ppermute(lax.slice_in_dim(block, 0, width, axis=dim), axis, backward)
        block = jnp.concatenate([low, block, high], axis=dim)
    return block


def edge_stacks(layout):
    column_edges = jnp.stack([layout[:, :EW], layout[:, EW : 2 * EW]])
    row_edges = jnp.stack([layout[:, 2 * EW : 2 * EW + ES], layout[:, 2 * EW + ES :]])
    return (column_edges, row_edges)


def add_edges(values, position, across, along):
    outside = jnp.concatenate([across[0], across[3], along[0], along[3]], axis=1)
    return values + jnp.take(outside, position, axis=1)


def assemble(values, position, inverse):
    column_edges, row_edges = edge_stacks(jnp.take(values, inverse, axis=1))
    across = padded(column_edges, (("gy", 0),), 1)
    along = padded(row_edges, (("gx", 0),), 1)
    return add_edges(values, position, across, along)


def per_device(schur_blocks, basis, loads, coarse_inverse, iface_map, coarse_slot):
    schur_block = schur_blocks[0, 0]
    local_basis = basis[0, 0]
    position = iface_map[0, 0]
    inverse = jnp.argsort(position)
    mode_count = local_basis.shape[0]
    domain_count = coarse_slot.shape[0]
    reordered = jnp.take(
        coarse_inverse.reshape(mode_count, domain_count, mode_count), coarse_slot, axis=1
    )
    reordered = reordered.reshape(mode_count, domain_count * mode_count)
    residual = assemble(loads[0, 0], position, inverse)
    solution = jnp.zeros_like(residual)
    for iteration in range(ITERS):
        lifted = lax.dot_general(
            lax.all_gather(
                lax.dot_general(
                    residual,
                    local_basis,
                    (((1,), (1,)), ((), ())),
                    precision=highest,
                    preferred_element_type=jnp.float32,
                ),
                ("gx", "gy"),
                axis=1,
                tiled=True,
            ),
            reordered,
            (((1,), (1,)), ((), ())),
            precision=highest,
            preferred_element_type=jnp.float32,
        )
        spread = jnp.dot(lifted, local_basis, precision=highest, preferred_element_type=jnp.float32)
        column_edges, row_edges = edge_stacks(jnp.take(spread, inverse, axis=1))
        across = padded(column_edges, (("gy", 0),), 1)
        along = padded(row_edges, (("gx", 0),), 1)
        search = residual + add_edges(spread, position, across, along)
        local_image = jnp.dot(
            search, schur_block, precision=highest, preferred_element_type=jnp.float32
        )
        applied = assemble(local_image, position, inverse)
        totals = lax.psum(
            (jnp.sum(residual * applied, axis=1), jnp.sum(applied * applied, axis=1)), ("gx", "gy")
        )
        stride = (totals[0] / (totals[1] + epsilon))[:, None]
        solution = solution + stride * search
        residual = residual - stride * applied
    return solution[None, None]


def solution(mesh):
    placed = (
        P("gx", "gy", None, None),
        P("gx", "gy", None, None),
        P("gx", "gy", None, None),
        P(("gx", "gy"), None),
        P("gx", "gy", None),
        P(),
    )
    return jax.shard_map(
        per_device, mesh=mesh, in_specs=placed, out_specs=P("gx", "gy", None, None), check_vma=False
    )
```

profile of v0, /device:TPU:1, one launch (start us, length us, event | category | flops | bytes accessed | tf_op | source)
XLA Modules:
  0.0 1102.9 jit_solution(14531170180641245100)
XLA Ops:
  7.4 4.4 sort.17
  14.6 4.4 collective-permute-start
  20.3 4.0 collective-permute-start.2
  24.3 2.9 collective-permute-start.3
  27.3 2.6 collective-permute-done.3
  32.6 6.4 reshape.19
  39.0 11.5 %copy.97 = f32[32,512,32]{2,0,1:T(8,128)} copy(f32[32,512,32]{2,1,0:T(8,128)} %reshape.19) | data formatting | bytes 4194304 | tf_op jit(solution)/shard_map/reshape | solution.py:52
  50.5 7.7 gather_fusion
  58.3 11.5 %copy.98 = f32[32,512,32]{2,1,0:T(8,128)} copy(f32[32,512,32]{2,0,1:T(8,128)} %bitcast.179) | data formatting | bytes 4194304 | tf_op jit(solution)/shard_map/jit(_take)/gather | solution.py:51
  69.8 7.4 gather.10
  78.1 160.3 %all-gather.7.cloned.1.call-done = f32[512,32,16]{1,2,0:T(8,128)} async-done(((f32[1,32,16]{1,2,0:T(8,128)}), f32[512,32,16]{1,2,0:T(8,128)}) %all-gather.7.cloned.1.call-update) | async-done | bytes 1048592 | tf_op jit(solution)/shard_map/all_gather | solution.py:59
  238.4 5.5 copy.96
  243.9 3.5 reshape.156
  247.4 3.3 fusion.10
  253.9 3.2 collective-permute-start.4
  258.4 3.4 collective-permute-start.6
  263.7 3.6 collective-permute-done.7
  272.4 4.3 collective-permute-start.8
  278.0 2.1 collective-permute-start.10
  280.2 2.2 collective-permute-start.11
  282.4 3.4 collective-permute-done.11
  287.6 106.4 %all-reduce.2 = (f32[16]{0:T(128)S(1)}, f32[16]{0:T(128)S(1)}) all-reduce(f32[16]{0:T(128)S(1)} %get-tuple-element.13, f32[16]{0:T(128)S(1)} %get-tuple-element.12), channel_id=1, replica_groups=mesh['gx'=32,'gy'=16] {'gx','gy'}, use_global_device_ids=true, to_apply=%region_2.4 | all-reduce | flops 32 | bytes 256 | tf_op jit(solution)/shard_map/psum | solution.py:85
  395.6 193.8 %all-gather.9.cloned.1.call-done = f32[512,32,16]{1,2,0:T(8,128)} async-done(((f32[1,32,16]{1,2,0:T(8,128)}), f32[512,32,16]{1,2,0:T(8,128)}) %all-gather.9.cloned.1.call-update) | async-done | bytes 1048592 | tf_op jit(solution)/shard_map/all_gather | solution.py:59
  589.5 5.6 copy.103
  595.0 3.7 reshape.158
  598.7 3.3 fusion.8
  604.3 3.0 collective-permute-start.12
  608.6 3.6 collective-permute-start.14
  612.2 1.9 collective-permute-start.15
  614.1 3.6 collective-permute-done.15
  622.7 4.3 collective-permute-start.16
  628.4 2.2 collective-permute-start.18
  630.5 2.2 collective-permute-start.19
  632.7 3.4 collective-permute-done.19
  638.0 106.4 %all-reduce.1 = (f32[16]{0:T(128)S(1)}, f32[16]{0:T(128)S(1)}) all-reduce(f32[16]{0:T(128)S(1)} %get-tuple-element.11, f32[16]{0:T(128)S(1)} %get-tuple-element.10), channel_id=1, replica_groups=mesh['gx'=32,'gy'=16] {'gx','gy'}, use_global_device_ids=true, to_apply=%region_6.8 | all-reduce | flops 32 | bytes 256 | tf_op jit(solution)/shard_map/psum | solution.py:85
  745.3 193.9 %all-gather.11.cloned.1.call-done = f32[512,32,16]{1,2,0:T(8,128)} async-done(((f32[1,32,16]{1,2,0:T(8,128)}), f32[512,32,16]{1,2,0:T(8,128)}) %all-gather.11.cloned.1.call-update) | async-done | bytes 1048592 | tf_op jit(solution)/shard_map/all_gather | solution.py:59
  939.2 5.6 copy.108
  944.8 3.5 reshape.160
  948.3 3.3 fusion.6
  954.7 3.0 collective-permute-start.20
  959.3 3.6 collective-permute-start.22
  962.9 1.9 collective-permute-start.23
  964.8 3.6 collective-permute-done.23
  973.5 4.3 collective-permute-start.24
  979.1 2.1 collective-permute-start.26
  981.2 2.2 collective-permute-start.27
  983.4 3.4 collective-permute-done.27
  988.7 106.4 %all-reduce = (f32[16]{0:T(128)S(1)}, f32[16]{0:T(128)S(1)}) all-reduce(f32[16]{0:T(128)S(1)} %get-tuple-element.9, f32[16]{0:T(128)S(1)} %get-tuple-element.8), channel_id=1, replica_groups=mesh['gx'=32,'gy'=16] {'gx','gy'}, use_global_device_ids=true, to_apply=%region_10.12 | all-reduce | flops 32 | bytes 256 | tf_op jit(solution)/shard_map/psum | solution.py:85
  (188 shorter events, 50.3 us)
Async XLA Ops:
  6.5 262.6 %copy-start = (f32[1,1,768,768]{3,2,1,0:T(8,128)S(1)}, f32[1,1,768,768]{3,2,1,0:T(8,128)}, u32[]{:S(2)}) copy-start(f32[1,1,768,768]{3,2,1,0:T(8,128)} %param.8) | copy-start | bytes 7077892
  6.5 25.1 %copy-start.17 = (f32[1,1,16,768]{3,2,1,0:T(8,128)S(1)}, f32[1,1,16,768]{3,2,1,0:T(8,128)}, u32[]{:S(2)}) copy-start(f32[1,1,16,768]{3,2,1,0:T(8,128)} %param.10) | copy-start | bytes 147460
  6.5 25.2 %copy-start.1 = (f32[1,1,32,768]{3,2,1,0:T(8,128)S(1)}, f32[1,1,32,768]{3,2,1,0:T(8,128)}, u32[]{:S(2)}) copy-start(f32[1,1,32,768]{3,2,1,0:T(8,128)} %param.9) | copy-start | bytes 294916
  6.5 231.9 %all-gather.7.cloned.1.call-start = ((), (), s32[]{:S(2)}) async-start(), calls=%async_computation | async-start | bytes 4202496 | tf_op jit(solution)/shard_map/all_gather | solution.py:59
  11.8 15.5 %copy-start.12 = (s32[1024]{0:T(1024)}, s32[1024]{0:T(1024)S(1)}, u32[]{:S(2)}) copy-start(s32[1024]{0:T(1024)S(1)} %pad_clamp_fusion.2) | copy-start | bytes 12292
  14.6 15.3 %collective-permute-start = (f32[1,16,256]{1,2,0:T(8,128)S(1)}, f32[1,16,256]{1,2,0:T(8,128)S(1)}, u32[]{:S(2)}, u32[]{:S(2)}) collective-permute-start(f32[1,16,256]{1,2,0:T(8,128)S(1)} %get-tuple-element.46), channel_id=1, source_target_pairs={{0,1},{1,2},{2,3},{3,4},{4,5},{5,6},{6,7},{7,8},{8,9},{9,10},{10,1... | collective-permute-start | bytes 49160 | tf_op jit(solution)/shard_map/ppermute | solution.py:18
  19.0 11.0 collective-permute-start.1
  20.3 7.1 collective-permute-start.2
  24.3 5.6 collective-permute-start.3
  32.5 556.9 %all-gather.9.cloned.1.call-start = ((), (), s32[]{:S(2)}) async-start(), calls=%async_computation.1 | async-start | bytes 4202496 | tf_op jit(solution)/shard_map/all_gather | solution.py:59
  250.8 16.7 %copy-start.9 = (s32[1024]{0:T(1024)S(1)}, s32[1024]{0:T(1024)}, u32[]{:S(2)}) copy-start(s32[1024]{0:T(1024)} %copy-done.8) | copy-start | bytes 12292
  250.8 18.4 %copy-start.19 = (pred[768]{0:T(1024)(128)(4,1)S(1)}, pred[768]{0:T(1024)(128)(4,1)}, u32[]{:S(2)}) copy-start(pred[768]{0:T(1024)(128)(4,1)} %copy-done.18) | copy-start | bytes 2308
  253.9 13.5 %collective-permute-start.4 = (f32[1,16,256]{1,2,0:T(8,128)S(1)}, f32[1,16,256]{1,2,0:T(8,128)S(1)}, u32[]{:S(2)}, u32[]{:S(2)}) collective-permute-start(f32[1,16,256]{1,2,0:T(8,128)S(1)} %get-tuple-element.42), channel_id=1, source_target_pairs={{0,1},{1,2},{2,3},{3,4},{4,5},{5,6},{6,7},{7,8},{8,9},{9,10},{10,1... | collective-permute-start | bytes 49160 | tf_op jit(solution)/shard_map/ppermute | solution.py:18
  257.0 10.3 collective-permute-start.5
  258.4 5.4 collective-permute-start.6
  261.8 5.6 collective-permute-start.7
  272.4 13.4 %collective-permute-start.8 = (f32[1,16,256]{1,2,0:T(8,128)S(1)}, f32[1,16,256]{1,2,0:T(8,128)S(1)}, u32[]{:S(2)}, u32[]{:S(2)}) collective-permute-start(f32[1,16,256]{1,2,0:T(8,128)S(1)} %get-tuple-element.38), channel_id=1, source_target_pairs={{0,1},{1,2},{2,3},{3,4},{4,5},{5,6},{6,7},{7,8},{8,9},{9,10},{10,1... | collective-permute-start | bytes 49160 | tf_op jit(solution)/shard_map/ppermute | solution.py:18
  276.7 9.1 collective-permute-start.9
  278.0 4.3 collective-permute-start.10
  280.2 5.6 collective-permute-start.11
  394.1 195.4 %copy-start.27 = (f32[16]{0:T(128)}, f32[16]{0:T(128)S(1)}, u32[]{:S(2)}) copy-start(f32[16]{0:T(128)S(1)} %add_divide_fusion.2) | copy-start | bytes 196
  395.6 543.6 %all-gather.11.cloned.1.call-start = ((), (), s32[]{:S(2)}) async-start(), calls=%async_computation.2 | async-start | bytes 4202496 | tf_op jit(solution)/shard_map/all_gather | solution.py:59
  602.1 15.7 %copy-start.10 = (s32[1024]{0:T(1024)S(1)}, s32[1024]{0:T(1024)}, u32[]{:S(2)}) copy-start(s32[1024]{0:T(1024)} %copy-done.8) | copy-start | bytes 12292
  602.1 17.5 %copy-start.3 = (f32[16,768]{1,0:T(8,128)S(1)}, f32[16,768]{1,0:T(8,128)}, u32[]{:S(2)}) copy-start(f32[16,768]{1,0:T(8,128)} %copy-done.2) | copy-start | bytes 147460
  602.1 17.4 %copy-start.20 = (pred[768]{0:T(1024)(128)(4,1)S(1)}, pred[768]{0:T(1024)(128)(4,1)}, u32[]{:S(2)}) copy-start(pred[768]{0:T(1024)(128)(4,1)} %copy-done.18) | copy-start | bytes 2308
  604.3 13.5 %collective-permute-start.12 = (f32[1,16,256]{1,2,0:T(8,128)S(1)}, f32[1,16,256]{1,2,0:T(8,128)S(1)}, u32[]{:S(2)}, u32[]{:S(2)}) collective-permute-start(f32[1,16,256]{1,2,0:T(8,128)S(1)} %get-tuple-element.34), channel_id=1, source_target_pairs={{0,1},{1,2},{2,3},{3,4},{4,5},{5,6},{6,7},{7,8},{8,9},{9,10},{10,1... | collective-permute-start | bytes 49160 | tf_op jit(solution)/shard_map/ppermute | solution.py:18
  607.3 10.5 collective-permute-start.13
  608.6 5.5 collective-permute-start.14
  612.2 5.6 collective-permute-start.15
  622.7 13.4 %collective-permute-start.16 = (f32[1,16,256]{1,2,0:T(8,128)S(1)}, f32[1,16,256]{1,2,0:T(8,128)S(1)}, u32[]{:S(2)}, u32[]{:S(2)}) collective-permute-start(f32[1,16,256]{1,2,0:T(8,128)S(1)} %get-tuple-element.30), channel_id=1, source_target_pairs={{0,1},{1,2},{2,3},{3,4},{4,5},{5,6},{6,7},{7,8},{8,9},{9,10},{10,1... | collective-permute-start | bytes 49160 | tf_op jit(solution)/shard_map/ppermute | solution.py:18
  627.0 9.1 collective-permute-start.17
  628.4 4.3 collective-permute-start.18
  630.5 5.6 collective-permute-start.19
  744.4 194.8 %copy-start.29 = (f32[16]{0:T(128)}, f32[16]{0:T(128)S(1)}, u32[]{:S(2)}) copy-start(f32[16]{0:T(128)S(1)} %add_divide_fusion.1) | copy-start | bytes 196
  951.6 16.9 %copy-start.11 = (s32[1024]{0:T(1024)S(1)}, s32[1024]{0:T(1024)}, u32[]{:S(2)}) copy-start(s32[1024]{0:T(1024)} %copy-done.8) | copy-start | bytes 12292
  951.8 18.4 %copy-start.21 = (pred[768]{0:T(1024)(128)(4,1)S(1)}, pred[768]{0:T(1024)(128)(4,1)}, u32[]{:S(2)}) copy-start(pred[768]{0:T(1024)(128)(4,1)} %copy-done.18) | copy-start | bytes 2308
  954.7 13.8 %collective-permute-start.20 = (f32[1,16,256]{1,2,0:T(8,128)S(1)}, f32[1,16,256]{1,2,0:T(8,128)S(1)}, u32[]{:S(2)}, u32[]{:S(2)}) collective-permute-start(f32[1,16,256]{1,2,0:T(8,128)S(1)} %get-tuple-element.26), channel_id=1, source_target_pairs={{0,1},{1,2},{2,3},{3,4},{4,5},{5,6},{6,7},{7,8},{8,9},{9,10},{10,1... | collective-permute-start | bytes 49160 | tf_op jit(solution)/shard_map/ppermute | solution.py:18
  957.8 10.7 collective-permute-start.21
  959.3 5.5 collective-permute-start.22
  962.9 5.6 collective-permute-start.23
  971.5 123.7 %copy-start.5 = (f32[16,768]{1,0:T(8,128)S(1)}, f32[16,768]{1,0:T(8,128)}, u32[]{:S(2)}) copy-start(f32[16,768]{1,0:T(8,128)} %copy-done.4) | copy-start | bytes 147460
  971.5 123.7 %copy-start.7 = (f32[16,768]{1,0:T(8,128)S(1)}, f32[16,768]{1,0:T(8,128)}, u32[]{:S(2)}) copy-start(f32[16,768]{1,0:T(8,128)} %copy-done.6) | copy-start | bytes 147460
  971.5 123.7 %copy-start.28 = (f32[16]{0:T(128)S(1)}, f32[16]{0:T(128)}, u32[]{:S(2)}) copy-start(f32[16]{0:T(128)} %copy-done.27) | copy-start | bytes 196
  971.5 123.7 %copy-start.30 = (f32[16]{0:T(128)S(1)}, f32[16]{0:T(128)}, u32[]{:S(2)}) copy-start(f32[16]{0:T(128)} %copy-done.29) | copy-start | bytes 196
  973.5 13.3 %collective-permute-start.24 = (f32[1,16,256]{1,2,0:T(8,128)S(1)}, f32[1,16,256]{1,2,0:T(8,128)S(1)}, u32[]{:S(2)}, u32[]{:S(2)}) collective-permute-start(f32[1,16,256]{1,2,0:T(8,128)S(1)} %get-tuple-element.22), channel_id=1, source_target_pairs={{0,1},{1,2},{2,3},{3,4},{4,5},{5,6},{6,7},{7,8},{8,9},{9,10},{10,1... | collective-permute-start | bytes 49160 | tf_op jit(solution)/shard_map/ppermute | solution.py:18
  977.8 9.1 collective-permute-start.25
  979.1 4.3 collective-permute-start.26
  981.2 5.6 collective-permute-start.27
  (14 other events, 84.6 us)
Sparse Core Ops, SparseCore 0:
  32.7 205.7 all-gather.6
  395.7 193.6 all-gather.8
  745.5 193.7 all-gather.10
where the time goes:
time: 1110 us; the launch traced here: 1100 us
  waiting for transfers between devices  572 us (52%)
  blocking collectives  319 us (29%)
  local copies, waits for them, and re-layouts  99.1 us (9%)
  starting transfers between devices  72 us (6%)
  matrix products  16.6 us (1%)
  between operations  14.7 us (1%)
    all_gather x3, waiting for transfers between devices, per_device(): lax.all_gather(lax.dot_general(residual, local_basis, (((1,), (1,)), ((),...  548 us
    psum x3, blocking collectives, per_device(): lax.psum((jnp.sum(residual * applied, axis=1), jnp.sum(applied * applied,...  319 us
    ppermute x14, starting transfers between devices, padded(): lax.ppermute(lax.slice_in_dim(block, block.shape[dim] - width, None, axis...  47.4 us
    gather x3, local copies, waits for them, and re-layouts, per_device(): jnp.take(coarse_inverse.reshape(mode_count, domain_count, mode_count), co...  26.6 us
    ppermute x14, starting transfers between devices, padded(): lax.ppermute(lax.slice_in_dim(block, 0, width, axis=dim), axis, backward)  24.5 us
    ppermute x14, waiting for transfers between devices, padded(): lax.ppermute(lax.slice_in_dim(block, 0, width, axis=dim), axis, backward)  23.7 us
  transfers between devices with their start and end apart: 31, of which 10 were waited for; matrix products, arithmetic and copies ran while one was open for 4% of the time, Pallas kernels for 0%

commit v1 on v0

--- a/solution.py
+++ b/solution.py
@@ -55,18 +55,24 @@
     residual = assemble(loads[0, 0], position, inverse)
     solution = jnp.zeros_like(residual)
     for iteration in range(ITERS):
+
+        def figure_run(xin):
+            return jnp.concatenate(
+                lax.all_to_all(
+                    jnp.stack([xin for _ in range(lax.axis_size(("gx", "gy")))]), ("gx", "gy"), 0, 0
+                ),
+                axis=1,
+            )
+
         lifted = lax.dot_general(
-            lax.all_gather(
+            figure_run(
                 lax.dot_general(
                     residual,
                     local_basis,
                     (((1,), (1,)), ((), ())),
                     precision=highest,
                     preferred_element_type=jnp.float32,
-                ),
-                ("gx", "gy"),
-                axis=1,
-                tiled=True,
+                )
             ),
             reordered,
             (((1,), (1,)), ((), ())),

time: 1110 us -> 737 us (0.66)
  waiting for transfers between devices: 572 us -> 27.5 us
  blocking collectives: 319 us -> 453 us
  starting transfers between devices: 72 us -> 107 us
  other arithmetic: 9.34 us -> 29.9 us
  between operations: 14.7 us -> 1.31 us
    all_gather x3 -> x0, waiting for transfers between devices: 548 us -> none  [per_device(): lax.all_gather(lax.dot_general(residual, local_basis, (((1,), (1,)), ((),...]
    all_to_all x0 -> x2, blocking collectives: none -> 142 us  [figure_run(): lax.all_to_all(jnp.stack([xin for _ in range(lax.axis_size(('gx', 'gy')))...]
    ppermute x14, waiting for transfers between devices: 23.7 us -> 1.12 us  [padded(): lax.ppermute(lax.slice_in_dim(block, 0, width, axis=dim), axis, backward)]
    all_to_all x0 -> x1, starting transfers between devices: none -> 22.5 us  [figure_run(): lax.all_to_all(jnp.stack([xin for _ in range(lax.axis_size(('gx', 'gy')))...]
    gather x3 -> x1, local copies, waits for them, and re-layouts: 26.6 us -> 7.86 us  [per_device(): jnp.take(coarse_inverse.reshape(mode_count, domain_count, mode_count), co...]
    all_to_all x0 -> x1, waiting for transfers between devices: none -> 17.8 us  [figure_run(): lax.all_to_all(jnp.stack([xin for _ in range(lax.axis_size(('gx', 'gy')))...]
    all_gather x3 -> x0, local copies, waits for them, and re-layouts: 16.6 us -> none  [per_device(): lax.all_gather(lax.dot_general(residual, local_basis, (((1,), (1,)), ((),...]
    all_to_all x0 -> x3, other arithmetic: none -> 13.1 us  [figure_run(): lax.all_to_all(jnp.stack([xin for _ in range(lax.axis_size(('gx', 'gy')))...]
  transfers between devices with their start and end apart: 31 -> 29, of which waited for: 10 -> 9; matrix products, arithmetic and copies ran while one was open for 4% -> 5% of each run, Pallas kernels for 0% -> 0%
where the time goes in v1:
time: 737 us; the launch traced here: 731 us
  blocking collectives  453 us (61%)
  starting transfers between devices  107 us (15%)
  local copies, waits for them, and re-layouts  97.1 us (13%)
  other arithmetic  29.9 us (4%)
  waiting for transfers between devices  27.5 us (4%)
  matrix products  14.7 us (2%)
    psum x3, blocking collectives, per_device(): lax.psum((jnp.sum(residual * applied, axis=1), jnp.sum(applied * applied,...  312 us
    all_to_all x2, blocking collectives, figure_run(): lax.all_to_all(jnp.stack([xin for _ in range(lax.axis_size(('gx', 'gy')))...  142 us
    ppermute x14, starting transfers between devices, padded(): lax.ppermute(lax.slice_in_dim(block, block.shape[dim] - width, None, axis...  49.7 us
    ppermute x14, starting transfers between devices, padded(): lax.ppermute(lax.slice_in_dim(block, 0, width, axis=dim), axis, backward)  34.9 us
    all_to_all x1, starting transfers between devices, figure_run(): lax.all_to_all(jnp.stack([xin for _ in range(lax.axis_size(('gx', 'gy')))...  22.5 us
    unnamed x68, local copies, waits for them, and re-layouts  21.9 us
    reshape x2, local copies, waits for them, and re-layouts, per_device(): coarse_inverse.reshape(mode_count, domain_count, mode_count)  17.9 us
    all_to_all x1, waiting for transfers between devices, figure_run(): lax.all_to_all(jnp.stack([xin for _ in range(lax.axis_size(('gx', 'gy')))...  17.8 us
  transfers between devices with their start and end apart: 29, of which 9 were waited for; matrix products, arithmetic and copies ran while one was open for 5% of the time, Pallas kernels for 0%

profile of v1, /device:TPU:1, one launch (start us, length us, event | category | flops | bytes accessed | tf_op | source)
XLA Modules:
  0.0 731.0 jit_solution(11007985685335491376)
XLA Ops:
  0.9 4.4 sort.17
  8.0 8.7 %collective-permute-start.3 = (f32[1,16,128]{1,2,0:T(8,128)S(1)}, f32[1,16,128]{1,2,0:T(8,128)S(1)}, u32[]{:S(2)}, u32[]{:S(2)}) collective-permute-start(f32[1,16,128]{1,2,0:T(8,128)S(1)} %get-tuple-element.49), channel_id=1, source_target_pairs={{16,0},{32,16},{48,32},{64,48},{80,64},{96,80},{112,96},{128,112},... | collective-permute-start | bytes 24584 | tf_op jit(solution)/shard_map/ppermute | solution.py:21
  20.0 4.0 collective-permute-start
  27.9 2.3 stack.66
  30.2 4.6 reshape.206
  34.8 22.5 %all-to-all-start = ((f32[512,1,512]{2,1,0:T(1,128)}), f32[512,1,512]{2,1,0:T(1,128)S(1)}, u32[]{:S(2)}, u32[]{:S(2)}) async-start(f32[512,1,512]{2,1,0:T(1,128)} %reshape.206), calls=%async_computation | async-start | bytes 2097152 | tf_op jit(solution)/shard_map/all_to_all | solution.py:61
  57.4 6.4 reshape.36
  63.7 11.5 %copy.210 = f32[32,512,32]{2,0,1:T(8,128)} copy(f32[32,512,32]{2,1,0:T(8,128)} %reshape.36) | data formatting | bytes 4194304 | tf_op jit(solution)/shard_map/reshape | solution.py:52
  75.9 7.9 %gather_fusion = f32[512,32,32]{2,1,0:T(8,128)} fusion(f32[32,512,32]{2,0,1:T(8,128)} %copy.210, s32[1024]{0:T(1024)} %pad_clamp_fusion), kind=kCustom, calls=%fused_computation.14 | custom fusion | bytes 4196352 | tf_op jit(solution)/shard_map/jit(_take)/gather | solution.py:51
  84.4 6.3 select_bitcast_fusion
  90.7 6.7 copy.211
  97.3 17.8 %all-to-all-done = f32[512,1,512]{2,1,0:T(1,128)S(1)} async-done(((f32[512,1,512]{2,1,0:T(1,128)}), f32[512,1,512]{2,1,0:T(1,128)S(1)}, u32[]{:S(2)}, u32[]{:S(2)}) %all-to-all-start) | async-done | bytes 1048608 | tf_op jit(solution)/shard_map/all_to_all | solution.py:61
  116.6 4.4 reduce.1
  121.0 2.5 reshape.207
  123.5 3.4 copy.209
  127.0 3.3 convolution_bitcast_fusion.2
  134.7 4.0 collective-permute-start.4
  138.7 3.4 collective-permute-start.7
  151.9 4.0 collective-permute-start.8
  155.9 2.3 collective-permute-start.11
  158.3 4.4 collective-permute-start.10
  165.9 103.9 %all-reduce.2 = (f32[16]{0:T(128)S(1)}, f32[16]{0:T(128)S(1)}) all-reduce(f32[16]{0:T(128)S(1)} %get-tuple-element.13, f32[16]{0:T(128)S(1)} %get-tuple-element.12), channel_id=1, replica_groups=mesh['gx'=32,'gy'=16] {'gx','gy'}, use_global_device_ids=true, to_apply=%region_2.4 | all-reduce | flops 32 | bytes 256 | tf_op jit(solution)/shard_map/psum | solution.py:91
  270.7 2.2 stack.75
  273.0 3.8 reshape.208
  276.8 71.1 %all_to_all.15 = f32[512,1,512]{2,1,0:T(1,128)} all-to-all(f32[512,1,512]{2,1,0:T(1,128)S(1)} %reshape.208), channel_id=1, replica_groups=mesh['gx'=32,'gy'=16] {'gx','gy'}, dimensions={0} | all-to-all | bytes 2097152 | tf_op jit(solution)/shard_map/all_to_all | solution.py:61
  347.9 4.4 reduce.2
  352.3 2.5 reshape.209
  354.8 3.2 copy.216
  358.0 3.3 convolution_bitcast_fusion.1
  364.9 4.0 collective-permute-start.12
  368.9 3.4 collective-permute-start.15
  382.0 4.0 collective-permute-start.16
  386.1 2.3 collective-permute-start.19
  388.4 4.5 collective-permute-start.18
  396.0 103.9 %all-reduce.1 = (f32[16]{0:T(128)S(1)}, f32[16]{0:T(128)S(1)}) all-reduce(f32[16]{0:T(128)S(1)} %get-tuple-element.11, f32[16]{0:T(128)S(1)} %get-tuple-element.10), channel_id=1, replica_groups=mesh['gx'=32,'gy'=16] {'gx','gy'}, use_global_device_ids=true, to_apply=%region_6.8 | all-reduce | flops 32 | bytes 256 | tf_op jit(solution)/shard_map/psum | solution.py:91
  500.5 2.2 stack.84
  502.7 3.8 reshape.210
  506.5 70.6 %all_to_all.16 = f32[512,1,512]{2,1,0:T(1,128)} all-to-all(f32[512,1,512]{2,1,0:T(1,128)S(1)} %reshape.210), channel_id=1, replica_groups=mesh['gx'=32,'gy'=16] {'gx','gy'}, dimensions={0} | all-to-all | bytes 2097152 | tf_op jit(solution)/shard_map/all_to_all | solution.py:61
  577.1 4.4 reduce.3
  581.5 2.5 reshape.211
  584.0 3.2 copy.222
  587.2 3.3 convolution_bitcast_fusion
  595.0 4.0 collective-permute-start.20
  599.0 3.4 collective-permute-start.23
  612.2 4.0 collective-permute-start.24
  616.2 2.3 collective-permute-start.27
  618.5 4.4 collective-permute-start.26
  626.2 103.9 %all-reduce = (f32[16]{0:T(128)S(1)}, f32[16]{0:T(128)S(1)}) all-reduce(f32[16]{0:T(128)S(1)} %get-tuple-element.9, f32[16]{0:T(128)S(1)} %get-tuple-element.8), channel_id=1, replica_groups=mesh['gx'=32,'gy'=16] {'gx','gy'}, use_global_device_ids=true, to_apply=%region_10.12 | all-reduce | flops 32 | bytes 256 | tf_op jit(solution)/shard_map/psum | solution.py:91
  (191 shorter events, 66.3 us)
Async XLA Ops:
  0.0 147.4 %copy-start = (f32[1,1,768,768]{3,2,1,0:T(8,128)S(1)}, f32[1,1,768,768]{3,2,1,0:T(8,128)}, u32[]{:S(2)}) copy-start(f32[1,1,768,768]{3,2,1,0:T(8,128)} %param.8) | copy-start | bytes 7077892
  0.0 27.7 %copy-start.17 = (f32[1,1,16,768]{3,2,1,0:T(8,128)S(1)}, f32[1,1,16,768]{3,2,1,0:T(8,128)}, u32[]{:S(2)}) copy-start(f32[1,1,16,768]{3,2,1,0:T(8,128)} %param.10) | copy-start | bytes 147460
  0.0 27.7 %copy-start.2 = (f32[1,1,32,768]{3,2,1,0:T(8,128)S(1)}, f32[1,1,32,768]{3,2,1,0:T(8,128)}, u32[]{:S(2)}) copy-start(f32[1,1,32,768]{3,2,1,0:T(8,128)} %param.9) | copy-start | bytes 294916
  5.3 13.5 %copy-start.22 = (pred[768]{0:T(1024)(128)(4,1)}, pred[768]{0:T(1024)(128)(4,1)S(1)}, u32[]{:S(2)}) copy-start(pred[768]{0:T(1024)(128)(4,1)S(1)} %compare_and_fusion.1) | copy-start | bytes 2308
  6.2 17.8 %copy-start.13 = (s32[1024]{0:T(1024)}, s32[1024]{0:T(1024)S(1)}, u32[]{:S(2)}) copy-start(s32[1024]{0:T(1024)S(1)} %pad_clamp_fusion.2) | copy-start | bytes 12292
  8.0 16.1 %collective-permute-start.3 = (f32[1,16,128]{1,2,0:T(8,128)S(1)}, f32[1,16,128]{1,2,0:T(8,128)S(1)}, u32[]{:S(2)}, u32[]{:S(2)}) collective-permute-start(f32[1,16,128]{1,2,0:T(8,128)S(1)} %get-tuple-element.49), channel_id=1, source_target_pairs={{16,0},{32,16},{48,32},{64,48},{80,64},{96,80},{112,96},{128,112},... | collective-permute-start | bytes 24584 | tf_op jit(solution)/shard_map/ppermute | solution.py:21
  16.8 7.3 %collective-permute-start.2 = (f32[1,16,128]{1,2,0:T(8,128)S(1)}, f32[1,16,128]{1,2,0:T(8,128)S(1)}, u32[]{:S(2)}, u32[]{:S(2)}) collective-permute-start(f32[1,16,128]{1,2,0:T(8,128)S(1)} %get-tuple-element.48), channel_id=1, source_target_pairs={{0,16},{16,32},{32,48},{48,64},{64,80},{80,96},{96,112},{112,128},... | collective-permute-start | bytes 24584 | tf_op jit(solution)/shard_map/ppermute | solution.py:18
  18.7 6.5 collective-permute-start.1
  20.0 5.9 collective-permute-start
  34.8 80.3 %all-to-all-start = ((f32[512,1,512]{2,1,0:T(1,128)}), f32[512,1,512]{2,1,0:T(1,128)S(1)}, u32[]{:S(2)}, u32[]{:S(2)}) async-start(f32[512,1,512]{2,1,0:T(1,128)} %reshape.206), calls=%async_computation | async-start | bytes 2097152 | tf_op jit(solution)/shard_map/all_to_all | solution.py:61
  63.7 11.5 %copy-start.26 = (s32[512]{0:T(512)S(1)}, s32[512]{0:T(512)}, u32[]{:S(2)}) copy-start(s32[512]{0:T(512)} %param.13) | copy-start | bytes 6148
  130.3 15.4 %copy-start.10 = (s32[1024]{0:T(1024)S(1)}, s32[1024]{0:T(1024)}, u32[]{:S(2)}) copy-start(s32[1024]{0:T(1024)} %copy-done.9) | copy-start | bytes 12292
  130.3 17.1 %copy-start.19 = (pred[768]{0:T(1024)(128)(4,1)S(1)}, pred[768]{0:T(1024)(128)(4,1)}, u32[]{:S(2)}) copy-start(pred[768]{0:T(1024)(128)(4,1)} %copy-done.18) | copy-start | bytes 2308
  133.4 12.2 %collective-permute-start.5 = (f32[1,16,256]{1,2,0:T(8,128)S(1)}, f32[1,16,256]{1,2,0:T(8,128)S(1)}, u32[]{:S(2)}, u32[]{:S(2)}) collective-permute-start(f32[1,16,256]{1,2,0:T(8,128)S(1)} %get-tuple-element.43), channel_id=1, source_target_pairs={{1,0},{2,1},{3,2},{4,3},{5,4},{6,5},{7,6},{8,7},{9,8},{10,9},{11,1... | collective-permute-start | bytes 49160 | tf_op jit(solution)/shard_map/ppermute | solution.py:21
  134.7 10.9 %collective-permute-start.4 = (f32[1,16,256]{1,2,0:T(8,128)S(1)}, f32[1,16,256]{1,2,0:T(8,128)S(1)}, u32[]{:S(2)}, u32[]{:S(2)}) collective-permute-start(f32[1,16,256]{1,2,0:T(8,128)S(1)} %get-tuple-element.42), channel_id=1, source_target_pairs={{0,1},{1,2},{2,3},{3,4},{4,5},{5,6},{6,7},{7,8},{8,9},{9,10},{10,1... | collective-permute-start | bytes 49160 | tf_op jit(solution)/shard_map/ppermute | solution.py:18
  138.7 5.6 collective-permute-start.7
  142.1 3.4 collective-permute-start.6
  147.4 8.5 %copy-start.5 = (f32[16,768]{1,0:T(8,128)}, f32[16,768]{1,0:T(8,128)S(1)}, u32[]{:S(2)}) copy-start(f32[16,768]{1,0:T(8,128)S(1)} %fusion.23) | copy-start | bytes 147460
  150.6 13.4 %collective-permute-start.9 = (f32[1,16,256]{1,2,0:T(8,128)S(1)}, f32[1,16,256]{1,2,0:T(8,128)S(1)}, u32[]{:S(2)}, u32[]{:S(2)}) collective-permute-start(f32[1,16,256]{1,2,0:T(8,128)S(1)} %get-tuple-element.39), channel_id=1, source_target_pairs={{1,0},{2,1},{3,2},{4,3},{5,4},{6,5},{7,6},{8,7},{9,8},{10,9},{11,1... | collective-permute-start | bytes 49160 | tf_op jit(solution)/shard_map/ppermute | solution.py:21
  151.9 12.1 %collective-permute-start.8 = (f32[1,16,256]{1,2,0:T(8,128)S(1)}, f32[1,16,256]{1,2,0:T(8,128)S(1)}, u32[]{:S(2)}, u32[]{:S(2)}) collective-permute-start(f32[1,16,256]{1,2,0:T(8,128)S(1)} %get-tuple-element.38), channel_id=1, source_target_pairs={{0,1},{1,2},{2,3},{3,4},{4,5},{5,6},{6,7},{7,8},{8,9},{9,10},{10,1... | collective-permute-start | bytes 49160 | tf_op jit(solution)/shard_map/ppermute | solution.py:18
  155.9 6.8 collective-permute-start.11
  158.3 5.7 collective-permute-start.10
  361.4 14.4 %copy-start.11 = (s32[1024]{0:T(1024)S(1)}, s32[1024]{0:T(1024)}, u32[]{:S(2)}) copy-start(s32[1024]{0:T(1024)} %copy-done.9) | copy-start | bytes 12292
  361.4 16.2 %copy-start.4 = (f32[16,768]{1,0:T(8,128)S(1)}, f32[16,768]{1,0:T(8,128)}, u32[]{:S(2)}) copy-start(f32[16,768]{1,0:T(8,128)} %copy-done.3) | copy-start | bytes 147460
  361.4 16.1 %copy-start.20 = (pred[768]{0:T(1024)(128)(4,1)S(1)}, pred[768]{0:T(1024)(128)(4,1)}, u32[]{:S(2)}) copy-start(pred[768]{0:T(1024)(128)(4,1)} %copy-done.18) | copy-start | bytes 2308
  363.6 12.2 %collective-permute-start.13 = (f32[1,16,256]{1,2,0:T(8,128)S(1)}, f32[1,16,256]{1,2,0:T(8,128)S(1)}, u32[]{:S(2)}, u32[]{:S(2)}) collective-permute-start(f32[1,16,256]{1,2,0:T(8,128)S(1)} %get-tuple-element.35), channel_id=1, source_target_pairs={{1,0},{2,1},{3,2},{4,3},{5,4},{6,5},{7,6},{8,7},{9,8},{10,9},{11,1... | collective-permute-start | bytes 49160 | tf_op jit(solution)/shard_map/ppermute | solution.py:21
  364.9 10.9 %collective-permute-start.12 = (f32[1,16,256]{1,2,0:T(8,128)S(1)}, f32[1,16,256]{1,2,0:T(8,128)S(1)}, u32[]{:S(2)}, u32[]{:S(2)}) collective-permute-start(f32[1,16,256]{1,2,0:T(8,128)S(1)} %get-tuple-element.34), channel_id=1, source_target_pairs={{0,1},{1,2},{2,3},{3,4},{4,5},{5,6},{6,7},{7,8},{8,9},{9,10},{10,1... | collective-permute-start | bytes 49160 | tf_op jit(solution)/shard_map/ppermute | solution.py:18
  368.9 5.6 collective-permute-start.15
  372.3 3.5 collective-permute-start.14
  377.6 8.5 %copy-start.7 = (f32[16,768]{1,0:T(8,128)}, f32[16,768]{1,0:T(8,128)S(1)}, u32[]{:S(2)}) copy-start(f32[16,768]{1,0:T(8,128)S(1)} %fusion.22) | copy-start | bytes 147460
  380.7 13.4 %collective-permute-start.17 = (f32[1,16,256]{1,2,0:T(8,128)S(1)}, f32[1,16,256]{1,2,0:T(8,128)S(1)}, u32[]{:S(2)}, u32[]{:S(2)}) collective-permute-start(f32[1,16,256]{1,2,0:T(8,128)S(1)} %get-tuple-element.31), channel_id=1, source_target_pairs={{1,0},{2,1},{3,2},{4,3},{5,4},{6,5},{7,6},{8,7},{9,8},{10,9},{11,1... | collective-permute-start | bytes 49160 | tf_op jit(solution)/shard_map/ppermute | solution.py:21
  382.0 12.1 %collective-permute-start.16 = (f32[1,16,256]{1,2,0:T(8,128)S(1)}, f32[1,16,256]{1,2,0:T(8,128)S(1)}, u32[]{:S(2)}, u32[]{:S(2)}) collective-permute-start(f32[1,16,256]{1,2,0:T(8,128)S(1)} %get-tuple-element.30), channel_id=1, source_target_pairs={{0,1},{1,2},{2,3},{3,4},{4,5},{5,6},{6,7},{7,8},{8,9},{9,10},{10,1... | collective-permute-start | bytes 49160 | tf_op jit(solution)/shard_map/ppermute | solution.py:18
  386.1 6.8 collective-permute-start.19
  388.4 5.8 collective-permute-start.18
  590.5 15.4 %copy-start.12 = (s32[1024]{0:T(1024)S(1)}, s32[1024]{0:T(1024)}, u32[]{:S(2)}) copy-start(s32[1024]{0:T(1024)} %copy-done.9) | copy-start | bytes 12292
  590.7 16.9 %copy-start.21 = (pred[768]{0:T(1024)(128)(4,1)S(1)}, pred[768]{0:T(1024)(128)(4,1)}, u32[]{:S(2)}) copy-start(pred[768]{0:T(1024)(128)(4,1)} %copy-done.18) | copy-start | bytes 2308
  593.7 12.2 %collective-permute-start.21 = (f32[1,16,256]{1,2,0:T(8,128)S(1)}, f32[1,16,256]{1,2,0:T(8,128)S(1)}, u32[]{:S(2)}, u32[]{:S(2)}) collective-permute-start(f32[1,16,256]{1,2,0:T(8,128)S(1)} %get-tuple-element.27), channel_id=1, source_target_pairs={{1,0},{2,1},{3,2},{4,3},{5,4},{6,5},{7,6},{8,7},{9,8},{10,9},{11,1... | collective-permute-start | bytes 49160 | tf_op jit(solution)/shard_map/ppermute | solution.py:21
  595.0 10.9 %collective-permute-start.20 = (f32[1,16,256]{1,2,0:T(8,128)S(1)}, f32[1,16,256]{1,2,0:T(8,128)S(1)}, u32[]{:S(2)}, u32[]{:S(2)}) collective-permute-start(f32[1,16,256]{1,2,0:T(8,128)S(1)} %get-tuple-element.26), channel_id=1, source_target_pairs={{0,1},{1,2},{2,3},{3,4},{4,5},{5,6},{6,7},{7,8},{8,9},{9,10},{10,1... | collective-permute-start | bytes 49160 | tf_op jit(solution)/shard_map/ppermute | solution.py:18
  599.0 5.6 collective-permute-start.23
  602.4 3.4 collective-permute-start.22
  608.9 121.2 %copy-start.6 = (f32[16,768]{1,0:T(8,128)S(1)}, f32[16,768]{1,0:T(8,128)}, u32[]{:S(2)}) copy-start(f32[16,768]{1,0:T(8,128)} %copy-done.5) | copy-start | bytes 147460
  608.9 121.2 %copy-start.8 = (f32[16,768]{1,0:T(8,128)S(1)}, f32[16,768]{1,0:T(8,128)}, u32[]{:S(2)}) copy-start(f32[16,768]{1,0:T(8,128)} %copy-done.7) | copy-start | bytes 147460
  608.9 121.2 %copy-start.28 = (f32[16]{0:T(128)S(1)}, f32[16]{0:T(128)}, u32[]{:S(2)}) copy-start(f32[16]{0:T(128)} %copy-done.27) | copy-start | bytes 196
  608.9 121.2 %copy-start.30 = (f32[16]{0:T(128)S(1)}, f32[16]{0:T(128)}, u32[]{:S(2)}) copy-start(f32[16]{0:T(128)} %copy-done.29) | copy-start | bytes 196
  610.9 13.4 %collective-permute-start.25 = (f32[1,16,256]{1,2,0:T(8,128)S(1)}, f32[1,16,256]{1,2,0:T(8,128)S(1)}, u32[]{:S(2)}, u32[]{:S(2)}) collective-permute-start(f32[1,16,256]{1,2,0:T(8,128)S(1)} %get-tuple-element.23), channel_id=1, source_target_pairs={{1,0},{2,1},{3,2},{4,3},{5,4},{6,5},{7,6},{8,7},{9,8},{10,9},{11,1... | collective-permute-start | bytes 49160 | tf_op jit(solution)/shard_map/ppermute | solution.py:21
  612.2 12.1 %collective-permute-start.24 = (f32[1,16,256]{1,2,0:T(8,128)S(1)}, f32[1,16,256]{1,2,0:T(8,128)S(1)}, u32[]{:S(2)}, u32[]{:S(2)}) collective-permute-start(f32[1,16,256]{1,2,0:T(8,128)S(1)} %get-tuple-element.22), channel_id=1, source_target_pairs={{0,1},{1,2},{2,3},{3,4},{4,5},{5,6},{6,7},{7,8},{8,9},{9,10},{10,1... | collective-permute-start | bytes 49160 | tf_op jit(solution)/shard_map/ppermute | solution.py:18
  616.2 6.8 collective-permute-start.27
  618.5 5.7 collective-permute-start.26
  (12 other events, 40.2 us)
